TPU v7x, 128 devices: a whole 4x4x4 slice. The times are simulated.
128 devices in a mesh: row: 8 (over z, core), col: 16 (over x, y).
Axes of the slice: x: 4, y: 4, z: 4, core: 2. Of those that a mesh axis runs over, the one named last changes fastest.
Arguments:
- nodes: bfloat16 [65536, 512], P(('row', 'col')), may hold values from -6 to 6
- cotangent: bfloat16 [65536, 512], P(('row', 'col')), may hold values from -6 to 6
- edge_source: int32 [262144], P(('row', 'col')), may hold values from 0 to 639
- edge_target: int32 [262144], P(('row', 'col')), may hold values from 0 to 511
- halo_lists: int32 [128, 4, 32], P(('row', 'col')), may hold values from 0 to 511
- pool_owner: int32 [65536], P(('row', 'col')), may hold values from 0 to 127, as said below
- pool_table: int32 [128, 1024], P(('row', 'col')), may hold values from -1 to 127, as said below
- source_weight: bfloat16 [512, 512], replicated, may hold values from -0.25 to 0.25
- target_weight: bfloat16 [512, 512], replicated, may hold values from -0.25 to 0.25
- edge_weight: bfloat16 [512, 512], replicated, may hold values from -0.25 to 0.25
- inner_weight: bfloat16 [1024, 512], replicated, may hold values from -0.1875 to 0.1875
- outer_weight: bfloat16 [512, 512], replicated, may hold values from -0.25 to 0.25
- coarse_weight: bfloat16 [512, 512], replicated, may hold values from -0.5 to 0.5
Outputs:
- updated: bfloat16 [65536, 512], P(('row', 'col'))
- node_gradient: float32 [65536, 512], P(('row', 'col'))
- source_gradient: float32 [512, 512], replicated
- target_gradient: float32 [512, 512], replicated
- edge_gradient: float32 [512, 512], replicated
- inner_gradient: float32 [1024, 512], replicated
- outer_gradient: float32 [512, 512], replicated
- coarse_gradient: float32 [512, 512], replicated
Inputs may be any that keep to these rules, and one draw needn't show every extreme that they name: `edge_source`: rows below 512 are the partition's own nodes; row 512 + k * 32 + j is row j of halo block k. `pool_owner`: at most 8 nodes of one partition name the same owner; one owner is named by exactly 8 nodes of every partition. `pool_table`: entry [o, q * 8 + k] is the coarse row of owner o for the node of rank k among the nodes of partition q that name o, and -1 where q names o fewer than k + 1 times.
All inputs are finite; a program needn't handle non-finite values.
Results may differ from a plain program's by a relative error of at most 0.014.
Values may be sent and summed in bfloat16 or wider, within the bound.
No kernel may reach another device: no remote copies, remote signals or barrier semaphores. Data moves between devices by JAX's collectives and lax.ppermute only.
A program may use at most 128 MiB of HBM per device.

v0:
```python
import math
import jax
import jax.numpy as jnp
from jax import lax
from jax.sharding import PartitionSpec as P


def passed_along(value, axis, steps):
    count = lax.axis_size(axis)
    initial, last = (max(0, -steps), min(count, count - steps))
    return lax.ppermute(value, axis, [(source, source + steps) for source in range(initial, last)])


def product(first, second):
    return jnp.dot(first, second, preferred_element_type=jnp.float32)


def left_product(first, second):
    return lax.dot_general(
        first, second, (((0,), (0,)), ((), ())), preferred_element_type=jnp.float32
    )


def right_product(first, second):
    return lax.dot_general(
        first, second, (((1,), (1,)), ((), ())), preferred_element_type=jnp.float32
    )


def silu_slope(value):
    sigma = jax.nn.sigmoid(value)
    return sigma * (1.0 + value * (1.0 - sigma))


def trade_halo(blocks, flip):
    moved = []
    for number, offset in enumerate((1, -1)):
        moved.append(passed_along(blocks[number], "row", offset * flip))
    for number, offset in enumerate((1, -1)):
        moved.append(passed_along(blocks[2 + number], "col", offset * flip))
    return moved


def trade_slots(buffer):
    return lax.all_to_all(buffer, ("row", "col"), split_axis=0, concat_axis=0, tiled=True)


def toward_owners(values, slot, devices, capacity, trader):
    width = values.shape[1]
    outgoing = jnp.zeros((devices * capacity, width), values.dtype).at[slot].set(values)
    arrived = trader(outgoing.reshape(devices, capacity, width))
    return arrived.reshape(devices * capacity, width)


def toward_sources(coarse_values, table, slot, devices, capacity, trader):
    width = coarse_values.shape[1]
    picked = jnp.take(coarse_values, jnp.maximum(table, 0), axis=0)
    picked = jnp.where((table >= 0)[:, None], picked, jnp.zeros_like(picked))
    returned = trader(picked.reshape(devices, capacity, width)).reshape(devices * capacity, width)
    return jnp.take(returned, slot, axis=0)


def local(
    nodes,
    cotangent,
    edge_source,
    edge_target,
    halo_lists,
    pool_owner,
    pool_table,
    source_weight,
    target_weight,
    edge_weight,
    inner_weight,
    outer_weight,
    coarse_weight,
):
    devices = lax.axis_size("row") * lax.axis_size("col")
    count_rows, width = nodes.shape
    lists = halo_lists[0]
    halo_rows = lists.shape[1]
    table = pool_table[0]
    capacity = table.shape[0] // devices
    coarse_rows = count_rows // 4
    scale = 1.0 / math.sqrt(count_rows * devices)
    received = trade_halo([jnp.take(nodes, lists[number], axis=0) for number in range(4)], 1)
    extended = jnp.concatenate([nodes] + received, axis=0)
    source_side = product(extended, source_weight)
    target_side = product(nodes, target_weight)
    edge_linear = jnp.take(source_side, edge_source, axis=0) + jnp.take(
        target_side, edge_target, axis=0
    )
    edge_hidden = jax.nn.silu(edge_linear).astype(jnp.bfloat16)
    message_linear = product(edge_hidden, edge_weight)
    aggregate = jax.ops.segment_sum(jax.nn.silu(message_linear), edge_target, count_rows).astype(
        jnp.bfloat16
    )
    joined = jnp.concatenate([nodes, aggregate], axis=1)
    node_linear = product(joined, inner_weight)
    node_hidden = jax.nn.silu(node_linear).astype(jnp.bfloat16)
    refined = (nodes.astype(jnp.float32) + product(node_hidden, outer_weight)).astype(jnp.bfloat16)
    owner_hot = (pool_owner[:, None] == jnp.arange(devices, dtype=jnp.int32)[None, :]).astype(
        jnp.bfloat16
    )
    positions = jnp.arange(count_rows, dtype=jnp.int32)
    lower = (positions[:, None] > positions[None, :]).astype(jnp.bfloat16)
    rank = jnp.sum(product(lower, owner_hot) * owner_hot, axis=1).astype(jnp.int32)
    slot = pool_owner * capacity + rank
    member = (jnp.arange(coarse_rows, dtype=jnp.int32)[:, None] == table[None, :]).astype(
        jnp.bfloat16
    )
    count = jnp.maximum(jnp.sum(member, axis=1, dtype=jnp.float32), 1.0)[:, None]
    arrived = toward_owners(refined, slot, devices, capacity, trade_slots)
    coarse = (product(member, arrived) / count).astype(jnp.bfloat16)
    coarse_linear = product(coarse, coarse_weight)
    coarse_update = jax.nn.silu(coarse_linear).astype(jnp.bfloat16)
    parent_rows = toward_sources(coarse_update, table, slot, devices, capacity, trade_slots)
    arrived_grad = toward_owners(cotangent, slot, devices, capacity, trade_slots)
    grad_coarse = (product(member, arrived_grad) * silu_slope(coarse_linear)).astype(jnp.bfloat16)
    coarse_share = (right_product(grad_coarse, coarse_weight) / count).astype(jnp.bfloat16)
    share_rows = toward_sources(coarse_share, table, slot, devices, capacity, trade_slots)
    updated = (refined.astype(jnp.float32) + parent_rows.astype(jnp.float32)).astype(jnp.bfloat16)
    coarse_gradient = left_product(coarse, grad_coarse)
    grad_refined = cotangent.astype(jnp.float32) + share_rows.astype(jnp.float32)
    refined_low = grad_refined.astype(jnp.bfloat16)
    outer_gradient = left_product(node_hidden, refined_low)
    grad_hidden = (right_product(refined_low, outer_weight) * silu_slope(node_linear)).astype(
        jnp.bfloat16
    )
    inner_gradient = left_product(joined, grad_hidden)
    grad_joined = right_product(grad_hidden, inner_weight)
    grad_aggregate = grad_joined[:, width:].astype(jnp.bfloat16)
    grad_message = (
        jnp.take(grad_aggregate, edge_target, axis=0) * silu_slope(message_linear)
    ).astype(jnp.bfloat16)
    edge_gradient = left_product(edge_hidden, grad_message)
    grad_edges = right_product(grad_message, edge_weight) * silu_slope(edge_linear)
    grad_sources = jax.ops.segment_sum(grad_edges, edge_source, extended.shape[0]).astype(
        jnp.bfloat16
    )
    grad_targets = jax.ops.segment_sum(grad_edges, edge_target, count_rows).astype(jnp.bfloat16)
    source_gradient = left_product(extended, grad_sources)
    target_gradient = left_product(nodes, grad_targets)
    (
        source_gradient,
        target_gradient,
        edge_gradient,
        inner_gradient,
        outer_gradient,
        coarse_gradient,
    ) = lax.psum(
        (
            source_gradient,
            target_gradient,
            edge_gradient,
            inner_gradient,
            outer_gradient,
            coarse_gradient,
        ),
        ("row", "col"),
    )
    grad_extended = right_product(grad_sources, source_weight)
    back_blocks = grad_extended[count_rows:].astype(jnp.bfloat16).reshape(4, halo_rows, width)
    returned = trade_halo([back_blocks[number] for number in range(4)], -1)
    node_gradient = (
        grad_refined
        + grad_joined[:, :width]
        + right_product(grad_targets, target_weight)
        + grad_extended[:count_rows]
    )
    node_gradient = node_gradient.at[lists.reshape(-1)].add(
        jnp.concatenate(returned, axis=0).astype(jnp.float32)
    )
    return (
        updated,
        node_gradient,
        source_gradient * scale,
        target_gradient * scale,
        edge_gradient * scale,
        inner_gradient * scale,
        outer_gradient * scale,
        coarse_gradient * scale,
    )


def solution(mesh):
    in_specs = (
        P(("row", "col"), None),
        P(("row", "col"), None),
        P(("row", "col")),
        P(("row", "col")),
        P(("row", "col"), None, None),
        P(("row", "col")),
        P(("row", "col"), None),
        P(),
        P(),
        P(),
        P(),
        P(),
        P(),
    )
    out_specs = (P(("row", "col"), None), P(("row", "col"), None), P(), P(), P(), P(), P(), P())
    return jax.shard_map(local, mesh=mesh, in_specs=in_specs, out_specs=out_specs, check_vma=False)
```

profile of v0, /device:TPU:1, one launch (start us, length us, event | category | flops | bytes accessed | tf_op | source)
XLA Modules:
  0.0 423.6 jit_solution(16720933355326291041)
XLA Ops:
  8.1 1.7 gather_fusion.3
  9.9 4.9 %collective-permute-start = (bf16[32,512]{1,0:T(8,128)(2,1)S(1)}, bf16[32,512]{1,0:T(8,128)(2,1)S(1)}, u32[]{:S(2)}, u32[]{:S(2)}) collective-permute-start(bf16[32,512]{1,0:T(8,128)(2,1)S(1)} %broadcast_select_fusion.4), channel_id=1, source_target_pairs={{0,16},{16,32},{32,48},{48,64},{64,80},{80,96},{96,112},{1,17},{17... | collective-permute-start | bytes 98312 | tf_op jit(solution)/shard_map/ppermute | solution.py:11
  14.8 1.7 gather_fusion.4
  16.7 1.9 collective-permute-start.1
  18.6 1.7 gather_fusion.5
  20.4 3.2 collective-permute-start.2
  23.6 1.7 gather_fusion.6
  25.5 1.3 collective-permute-start.3
  27.5 1.3 compare_and_fusion
  28.8 1.6 fusion.57
  30.4 1.1 fusion.9
  32.1 8.9 %gather_fusion.1 = f32[2048,512]{1,0:T(8,128)} fusion(f32[512,512]{1,0:T(8,128)S(1)} %fusion.57, s32[2048]{0:T(1024)S(1)} %get-tuple-element.46), kind=kCustom, calls=%fused_computation.9 | custom fusion | bytes 8396800 | tf_op jit(solution)/shard_map/jit(_take)/gather | solution.py:90
  41.1 1.5 fusion.56
  42.6 8.9 %gather_fusion = f32[2048,512]{1,0:T(8,128)} fusion(f32[640,512]{1,0:T(8,128)S(1)} %fusion.56, s32[2048]{0:T(1024)S(1)} %get-tuple-element.45), kind=kCustom, calls=%fused_computation.8 | custom fusion | bytes 8396800 | tf_op jit(solution)/shard_map/jit(_take)/gather | solution.py:90
  51.6 4.2 %multiply_convert_fusion.1 = bf16[2048,512]{1,0:T(8,128)(2,1)S(1)} fusion(f32[2048,512]{1,0:T(8,128)} %gather_fusion.1, pred[2048]{0:T(1024)(128)(4,1)} %get-tuple-element.47, f32[2048,512]{1,0:T(8,128)} %gather_fusion, pred[2048]{0:T(1024)(128)(4,1)} %get-tuple-element.48), kind=kLoop, calls=%fused_computation.22 | loop fusion | flops 8388608 | bytes 10489856 | tf_op jit(solution)/shard_map/convert_element_type | solution.py:93
  55.8 1.3 copy-done.5
  57.1 3.3 fusion.58
  60.4 14.6 %scatter_custom_fusion = f32[512,512]{1,0:T(8,128)S(1)} fusion(s32[2048]{0:T(1024)} %param.22, f32[2048,512]{1,0:T(8,128)} %fusion.58, f32[]{:T(128)} %constant.62.clone.1, f32[]{:T(128)} %constant.52.clone.1), kind=kCustom, calls=%fused_computation.19 | custom fusion | flops 5242880 | bytes 5243904 | tf_op jit(solution)/shard_map/scatter-add | solution.py:95
  77.2 3.6 scatter_custom_fusion.1
  80.8 11.6 %all-to-all-start = ((bf16[128,8,512]{2,1,0:T(8,128)(2,1)}), bf16[128,8,512]{2,1,0:T(8,128)(2,1)S(1)}, u32[]{:S(2)}, u32[]{:S(2)}) async-start(bf16[128,8,512]{2,1,0:T(8,128)(2,1)} %bitcast.5), calls=%async_computation | async-start | bytes 2097152 | tf_op jit(solution)/shard_map/all_to_all | solution.py:45
  92.4 4.0 scatter_custom_fusion.2
  96.4 14.7 %all-to-all-done = bf16[128,8,512]{2,1,0:T(8,128)(2,1)S(1)} async-done(((bf16[128,8,512]{2,1,0:T(8,128)(2,1)}), bf16[128,8,512]{2,1,0:T(8,128)(2,1)S(1)}, u32[]{:S(2)}, u32[]{:S(2)}) %all-to-all-start) | async-done | bytes 1048608 | tf_op jit(solution)/shard_map/all_to_all | solution.py:45
  111.2 5.7 %all-to-all-start.2 = ((bf16[128,8,512]{2,1,0:T(8,128)(2,1)}), bf16[128,8,512]{2,1,0:T(8,128)(2,1)}, u32[]{:S(2)}, u32[]{:S(2)}) async-start(bf16[128,8,512]{2,1,0:T(8,128)(2,1)} %bitcast.9), calls=%async_computation.2 | async-start | bytes 2097152 | tf_op jit(solution)/shard_map/all_to_all | solution.py:45
  117.8 1.4 multiply_convert_fusion.3
  119.2 16.3 %all-to-all-done.2 = bf16[128,8,512]{2,1,0:T(8,128)(2,1)} async-done(((bf16[128,8,512]{2,1,0:T(8,128)(2,1)}), bf16[128,8,512]{2,1,0:T(8,128)(2,1)}, u32[]{:S(2)}, u32[]{:S(2)}) %all-to-all-start.2) | async-done | bytes 1048608 | tf_op jit(solution)/shard_map/all_to_all | solution.py:45
  135.5 1.5 fusion.8
  137.7 1.4 fusion.6
  139.1 4.0 gather_fusion.9
  143.1 5.1 %gather_fusion.7 = bf16[1024,512]{1,0:T(8,128)(2,1)} fusion(bf16[128,512]{1,0:T(8,128)(2,1)S(1)} %get-tuple-element.41, s32[1024]{0:T(1024)S(1)} %maximum_clamp_fusion), kind=kCustom, calls=%fused_computation.1.clone | custom fusion | bytes 2101248 | tf_op jit(solution)/shard_map/jit(_take)/gather | solution.py:57
  148.2 2.9 fusion.12
  151.1 4.8 %all-to-all-start.3 = ((bf16[128,8,512]{2,1,0:T(8,128)(2,1)}), bf16[128,8,512]{2,1,0:T(8,128)(2,1)S(1)}, u32[]{:S(2)}, u32[]{:S(2)}) async-start(bf16[128,8,512]{2,1,0:T(8,128)(2,1)} %get-tuple-element.33), calls=%async_computation.3 | async-start | bytes 2097152 | tf_op jit(solution)/shard_map/all_to_all | solution.py:45
  156.0 2.3 fusion.61
  158.3 16.6 %all-to-all-done.3 = bf16[128,8,512]{2,1,0:T(8,128)(2,1)S(1)} async-done(((bf16[128,8,512]{2,1,0:T(8,128)(2,1)}), bf16[128,8,512]{2,1,0:T(8,128)(2,1)S(1)}, u32[]{:S(2)}, u32[]{:S(2)}) %all-to-all-start.3) | async-done | bytes 1048608 | tf_op jit(solution)/shard_map/all_to_all | solution.py:45
  174.9 2.6 gather_fusion.10
  177.5 2.4 fusion.5
  180.7 1.3 copy-done.8
  182.1 9.2 %gather_fusion.2 = bf16[2048,512]{1,0:T(8,128)(2,1)} fusion(bf16[512,512]{1,0:T(8,128)(2,1)S(1)} %slice.97, s32[2048]{0:T(1024)S(1)} %get-tuple-element.46), kind=kCustom, calls=%fused_computation.10 | custom fusion | bytes 4202496 | tf_op jit(solution)/shard_map/jit(_take)/gather | solution.py:134
  191.3 3.8 multiply_convert_fusion
  195.1 1.3 copy-done.10
  197.4 4.3 %multiply_multiply_fusion = f32[2048,512]{1,0:T(8,128)} fusion(bf16[2048,512]{1,0:T(8,128)(2,1)S(1)} %multiply_convert_fusion, bf16[512,512]{1,0:T(8,128)(2,1)S(1)} %copy-done.20, f32[2048,512]{1,0:T(8,128)S(1)} %copy-done.2, pred[2048]{0:T(1024)(128)(4,1)S(1)} %copy-done.31, f32[2048,512]{1,0:T(8,128)S(1)} %copy-done.3, pred[2048]{0:T(1024)(128)(4,1)S(1)} %copy-done.32), kind=kOutput, calls=%fused_computation.17 | convolution fusion | flops 1085276160 | bytes 15208448 | tf_op jit(solution)/shard_map/dot_general | solution.py:25
  201.6 13.6 %scatter_custom_fusion.4 = f32[640,512]{1,0:T(8,128)S(1)} fusion(s32[2048]{0:T(1024)} %param.21, f32[2048,512]{1,0:T(8,128)} %multiply_multiply_fusion, f32[]{:T(128)} %constant.52.clone.1), kind=kCustom, calls=%fused_computation.59 | custom fusion | flops 1048576 | bytes 1311232 | tf_op jit(solution)/shard_map/scatter-add | solution.py:138
  215.2 13.7 %scatter_custom_fusion.3 = f32[512,512]{1,0:T(8,128)S(1)} fusion(s32[2048]{0:T(1024)} %param.22, f32[2048,512]{1,0:T(8,128)} %multiply_multiply_fusion, f32[]{:T(128)} %constant.52.clone.1), kind=kCustom, calls=%fused_computation.73 | custom fusion | flops 1048576 | bytes 1049088 | tf_op jit(solution)/shard_map/scatter-add | solution.py:141
  229.0 4.9 %fusion.60 = f32[512,512]{1,0:T(8,128)} fusion(bf16[2048,512]{1,0:T(8,128)(2,1)} %copy-done.5, bf16[2048,512]{1,0:T(8,128)(2,1)} %copy-done.10), kind=kOutput, calls=%fused_computation.144 | convolution fusion | flops 1073741824 | bytes 5242880 | tf_op jit(solution)/shard_map/dot_general | solution.py:19
  233.9 2.1 fusion.15
  236.0 1.7 fusion.51
  237.6 1.6 fusion.27
  239.2 1.5 convolution_bitcast_fusion
  240.7 4.7 %all-to-all-start.1 = ((bf16[128,8,512]{2,1,0:T(8,128)(2,1)}), bf16[128,8,512]{2,1,0:T(8,128)(2,1)S(1)}, u32[]{:S(2)}, u32[]{:S(2)}) async-start(bf16[128,8,512]{2,1,0:T(8,128)(2,1)} %get-tuple-element.34), calls=%async_computation.1 | async-start | bytes 2097152 | tf_op jit(solution)/shard_map/all_to_all | solution.py:45
  245.5 22.7 %all-to-all-done.1 = bf16[128,8,512]{2,1,0:T(8,128)(2,1)S(1)} async-done(((bf16[128,8,512]{2,1,0:T(8,128)(2,1)}), bf16[128,8,512]{2,1,0:T(8,128)(2,1)S(1)}, u32[]{:S(2)}, u32[]{:S(2)}) %all-to-all-start.1) | async-done | bytes 1048608 | tf_op jit(solution)/shard_map/all_to_all | solution.py:45
  268.2 2.0 gather_fusion.8
  270.3 1.7 fusion.55
  272.0 2.4 collective-permute-start.7
  274.4 1.3 collective-permute-start.6
  275.7 3.1 collective-permute-start.5
  278.8 1.9 collective-permute-start.4
  280.8 1.6 fusion.3
  284.1 1.8 scatter_custom_fusion.5
  285.9 121.3 %all-reduce.3.cloned.1.call-done = (f32[512,512]{1,0:T(8,128)}, f32[512,512]{1,0:T(8,128)}, f32[512,512]{1,0:T(8,128)}, f32[1024,512]{1,0:T(8,128)}, f32[512,512]{1,0:T(8,128)}, /*index=5*/f32[512,512]{1,0:T(8,128)}) async-done(((f32[512,512]{1,0:T(8,128)}, f32[512,512]{1,0:T(8,128)}, f32[512,512]{1,0:T(8,128)}, f32[1024,512]{1,0:T(8,128)}, f32[512,512]{1,0:T(8,128)}, /*index=5*/f32[512,512]{1,0:T(8,128)}), ...) | async-done | bytes 7340048 | tf_op jit(solution)/shard_map/psum | solution.py:151
  407.2 2.4 broadcast_multiply_fusion.5
  409.6 2.4 broadcast_multiply_fusion.4
  412.0 1.1 broadcast_multiply_fusion.3
  413.1 1.5 broadcast_multiply_fusion
  414.6 1.1 broadcast_multiply_fusion.2
  415.7 1.1 broadcast_multiply_fusion.1
  (126 shorter events, 10.1 us)
Async XLA Ops:
  7.2 68.0 %copy-start = (bf16[1024,512]{1,0:T(8,128)(2,1)S(1)}, bf16[1024,512]{1,0:T(8,128)(2,1)}, u32[]{:S(2)}) copy-start(bf16[1024,512]{1,0:T(8,128)(2,1)} %param.29) | copy-start | bytes 3145732
  7.2 24.9 %copy-start.4 = (bf16[512,512]{1,0:T(8,128)(2,1)S(1)}, bf16[512,512]{1,0:T(8,128)(2,1)}, u32[]{:S(2)}) copy-start(bf16[512,512]{1,0:T(8,128)(2,1)} %param.19) | copy-start | bytes 1572868
  7.2 24.3 %copy-start.39 = (s32[512]{0:T(512)S(1)}, s32[512]{0:T(512)}, u32[]{:S(2)}) copy-start(s32[512]{0:T(512)} %param.24) | copy-start | bytes 6148
  9.9 31.1 %collective-permute-start = (bf16[32,512]{1,0:T(8,128)(2,1)S(1)}, bf16[32,512]{1,0:T(8,128)(2,1)S(1)}, u32[]{:S(2)}, u32[]{:S(2)}) collective-permute-start(bf16[32,512]{1,0:T(8,128)(2,1)S(1)} %broadcast_select_fusion.4), channel_id=1, source_target_pairs={{0,16},{16,32},{32,48},{48,64},{64,80},{80,96},{96,112},{1,17},{17... | collective-permute-start | bytes 98312 | tf_op jit(solution)/shard_map/ppermute | solution.py:11
  16.7 24.4 %collective-permute-start.1 = (bf16[32,512]{1,0:T(8,128)(2,1)S(1)}, bf16[32,512]{1,0:T(8,128)(2,1)S(1)}, u32[]{:S(2)}, u32[]{:S(2)}) collective-permute-start(bf16[32,512]{1,0:T(8,128)(2,1)S(1)} %broadcast_select_fusion.3), channel_id=1, source_target_pairs={{16,0},{32,16},{48,32},{64,48},{80,64},{96,80},{112,96},{17,1},{33... | collective-permute-start | bytes 98312 | tf_op jit(solution)/shard_map/ppermute | solution.py:11
  20.4 20.6 %collective-permute-start.2 = (bf16[32,512]{1,0:T(8,128)(2,1)S(1)}, bf16[32,512]{1,0:T(8,128)(2,1)S(1)}, u32[]{:S(2)}, u32[]{:S(2)}) collective-permute-start(bf16[32,512]{1,0:T(8,128)(2,1)S(1)} %broadcast_select_fusion.2), channel_id=1, source_target_pairs={{0,1},{1,2},{2,3},{3,4},{4,5},{5,6},{6,7},{7,8},{8,9},{9,10},{10,1... | collective-permute-start | bytes 98312 | tf_op jit(solution)/shard_map/ppermute | solution.py:11
  25.5 15.6 %collective-permute-start.3 = (bf16[32,512]{1,0:T(8,128)(2,1)S(1)}, bf16[32,512]{1,0:T(8,128)(2,1)S(1)}, u32[]{:S(2)}, u32[]{:S(2)}) collective-permute-start(bf16[32,512]{1,0:T(8,128)(2,1)S(1)} %broadcast_select_fusion.1), channel_id=1, source_target_pairs={{1,0},{2,1},{3,2},{4,3},{5,4},{6,5},{7,6},{8,7},{9,8},{10,9},{11,1... | collective-permute-start | bytes 98312 | tf_op jit(solution)/shard_map/ppermute | solution.py:11
  51.6 5.5 %copy-start.19 = (bf16[512,512]{1,0:T(8,128)(2,1)S(1)}, bf16[512,512]{1,0:T(8,128)(2,1)}, u32[]{:S(2)}) copy-start(bf16[512,512]{1,0:T(8,128)(2,1)} %param.28) | copy-start | bytes 1572868
  55.8 1.3 copy-start.5
  75.1 1.2 copy-start.40
  75.2 1.5 copy-start.22
  76.2 1.0 copy-start.42
  76.2 20.1 %copy-start.30 = (s32[1,1024]{1,0:T(1,128)S(1)}, s32[1,1024]{1,0:T(1,128)}, u32[]{:S(2)}) copy-start(s32[1,1024]{1,0:T(1,128)} %param.25) | copy-start | bytes 12292
  77.2 3.6 copy-start.26
  80.8 30.4 %all-to-all-start = ((bf16[128,8,512]{2,1,0:T(8,128)(2,1)}), bf16[128,8,512]{2,1,0:T(8,128)(2,1)S(1)}, u32[]{:S(2)}, u32[]{:S(2)}) async-start(bf16[128,8,512]{2,1,0:T(8,128)(2,1)} %bitcast.5), calls=%async_computation | async-start | bytes 2097152 | tf_op jit(solution)/shard_map/all_to_all | solution.py:45
  111.2 24.4 %all-to-all-start.2 = ((bf16[128,8,512]{2,1,0:T(8,128)(2,1)}), bf16[128,8,512]{2,1,0:T(8,128)(2,1)}, u32[]{:S(2)}, u32[]{:S(2)}) async-start(bf16[128,8,512]{2,1,0:T(8,128)(2,1)} %bitcast.9), calls=%async_computation.2 | async-start | bytes 2097152 | tf_op jit(solution)/shard_map/all_to_all | solution.py:45
  116.9 18.6 %copy-start.41 = (f32[128]{0:T(128)}, f32[128]{0:T(128)S(1)}, u32[]{:S(2)}) copy-start(f32[128]{0:T(128)S(1)} %broadcast_maximum_fusion) | copy-start | bytes 1540
  117.8 19.2 %copy-start.28 = (bf16[128,512]{1,0:T(8,128)(2,1)}, bf16[128,512]{1,0:T(8,128)(2,1)S(1)}, u32[]{:S(2)}) copy-start(bf16[128,512]{1,0:T(8,128)(2,1)S(1)} %fusion.7) | copy-start | bytes 393220
  137.1 0.7 copy-start.29
  143.1 5.1 %copy-start.37 = (pred[1024]{0:T(1024)(128)(4,1)S(1)}, pred[1024]{0:T(1024)(128)(4,1)}, u32[]{:S(2)}) copy-start(pred[1024]{0:T(1024)(128)(4,1)} %get-tuple-element.31) | copy-start | bytes 3076
  143.1 5.1 %copy-start.38 = (pred[1024]{0:T(1024)(128)(4,1)S(1)}, pred[1024]{0:T(1024)(128)(4,1)}, u32[]{:S(2)}) copy-start(pred[1024]{0:T(1024)(128)(4,1)} %get-tuple-element.32) | copy-start | bytes 3076
  148.2 7.8 %copy-start.34 = (s32[512]{0:T(512)S(1)}, s32[512]{0:T(512)}, u32[]{:S(2)}) copy-start(s32[512]{0:T(512)} %get-tuple-element.18) | copy-start | bytes 6148
  151.1 26.4 %copy-start.35 = (pred[512]{0:T(512)(128)(4,1)S(1)}, pred[512]{0:T(512)(128)(4,1)}, u32[]{:S(2)}) copy-start(pred[512]{0:T(512)(128)(4,1)} %get-tuple-element.17) | copy-start | bytes 1540
  151.1 23.8 %all-to-all-start.3 = ((bf16[128,8,512]{2,1,0:T(8,128)(2,1)}), bf16[128,8,512]{2,1,0:T(8,128)(2,1)S(1)}, u32[]{:S(2)}, u32[]{:S(2)}) async-start(bf16[128,8,512]{2,1,0:T(8,128)(2,1)} %get-tuple-element.33), calls=%async_computation.3 | async-start | bytes 2097152 | tf_op jit(solution)/shard_map/all_to_all | solution.py:45
  155.9 251.3 %all-reduce.3.cloned.1.call-start = ((), (), s32[]{:S(2)}) async-start(), calls=%async_computation.4 | async-start | bytes 14680064 | tf_op jit(solution)/shard_map/psum | solution.py:151
  179.9 0.8 copy-start.24
  180.7 1.3 copy-start.8
  182.1 9.2 %copy-start.31 = (pred[2048]{0:T(1024)(128)(4,1)S(1)}, pred[2048]{0:T(1024)(128)(4,1)}, u32[]{:S(2)}) copy-start(pred[2048]{0:T(1024)(128)(4,1)} %get-tuple-element.47) | copy-start | bytes 6148
  182.1 14.4 %copy-start.20 = (bf16[512,512]{1,0:T(8,128)(2,1)S(1)}, bf16[512,512]{1,0:T(8,128)(2,1)}, u32[]{:S(2)}) copy-start(bf16[512,512]{1,0:T(8,128)(2,1)} %param.28) | copy-start | bytes 1572868
  191.3 5.1 %copy-start.2 = (f32[2048,512]{1,0:T(8,128)S(1)}, f32[2048,512]{1,0:T(8,128)}, u32[]{:S(2)}) copy-start(f32[2048,512]{1,0:T(8,128)} %gather_fusion.1) | copy-start | bytes 12582916
  191.3 6.1 %copy-start.3 = (f32[2048,512]{1,0:T(8,128)S(1)}, f32[2048,512]{1,0:T(8,128)}, u32[]{:S(2)}) copy-start(f32[2048,512]{1,0:T(8,128)} %gather_fusion) | copy-start | bytes 12582916
  191.3 6.1 %copy-start.32 = (pred[2048]{0:T(1024)(128)(4,1)S(1)}, pred[2048]{0:T(1024)(128)(4,1)}, u32[]{:S(2)}) copy-start(pred[2048]{0:T(1024)(128)(4,1)} %get-tuple-element.48) | copy-start | bytes 6148
  195.1 1.3 copy-start.10
  228.9 10.3 %copy-start.6 = (f32[512,512]{1,0:T(8,128)}, f32[512,512]{1,0:T(8,128)S(1)}, u32[]{:S(2)}) copy-start(f32[512,512]{1,0:T(8,128)S(1)} %scatter_custom_fusion.3) | copy-start | bytes 3145732
  228.9 4.9 %copy-start.23 = (bf16[512,512]{1,0:T(8,128)(2,1)S(1)}, bf16[512,512]{1,0:T(8,128)(2,1)}, u32[]{:S(2)}) copy-start(bf16[512,512]{1,0:T(8,128)(2,1)} %copy-done.22) | copy-start | bytes 1572868
  228.9 4.9 %copy-start.25 = (bf16[512,512]{1,0:T(8,128)(2,1)S(1)}, bf16[512,512]{1,0:T(8,128)(2,1)}, u32[]{:S(2)}) copy-start(bf16[512,512]{1,0:T(8,128)(2,1)} %copy-done.24) | copy-start | bytes 1572868
  229.0 7.0 %copy-start.11 = (bf16[512,512]{1,0:T(8,128)(2,1)S(1)}, bf16[512,512]{1,0:T(8,128)(2,1)}, u32[]{:S(2)}) copy-start(bf16[512,512]{1,0:T(8,128)(2,1)} %gather_fusion.10) | copy-start | bytes 1572868
  229.0 7.0 %copy-start.21 = (bf16[512,512]{1,0:T(8,128)(2,1)S(1)}, bf16[512,512]{1,0:T(8,128)(2,1)}, u32[]{:S(2)}) copy-start(bf16[512,512]{1,0:T(8,128)(2,1)} %param.20) | copy-start | bytes 1572868
  229.0 7.0 %copy-start.36 = (pred[512]{0:T(512)(128)(4,1)S(1)}, pred[512]{0:T(512)(128)(4,1)}, u32[]{:S(2)}) copy-start(pred[512]{0:T(512)(128)(4,1)} %get-tuple-element.17) | copy-start | bytes 1540
  229.0 7.0 %copy-start.43 = (f32[512,512]{1,0:T(8,128)S(1)}, f32[512,512]{1,0:T(8,128)}, u32[]{:S(2)}) copy-start(f32[512,512]{1,0:T(8,128)} %copy-done.42) | copy-start | bytes 3145732
  240.7 4.7 %copy-start.33 = (s32[1,4,32]{2,1,0:T(4,128)S(1)}, s32[1,4,32]{2,1,0:T(4,128)}, u32[]{:S(2)}) copy-start(s32[1,4,32]{2,1,0:T(4,128)} %param.23) | copy-start | bytes 1540
  240.7 27.5 %all-to-all-start.1 = ((bf16[128,8,512]{2,1,0:T(8,128)(2,1)}), bf16[128,8,512]{2,1,0:T(8,128)(2,1)S(1)}, u32[]{:S(2)}, u32[]{:S(2)}) async-start(bf16[128,8,512]{2,1,0:T(8,128)(2,1)} %get-tuple-element.34), calls=%async_computation.1 | async-start | bytes 2097152 | tf_op jit(solution)/shard_map/all_to_all | solution.py:45
  268.2 12.5 %copy-start.12 = (bf16[512,512]{1,0:T(8,128)(2,1)S(1)}, bf16[512,512]{1,0:T(8,128)(2,1)}, u32[]{:S(2)}) copy-start(bf16[512,512]{1,0:T(8,128)(2,1)} %gather_fusion.10) | copy-start | bytes 1572868
  270.2 10.6 %copy-start.7 = (f32[512,512]{1,0:T(8,128)S(1)}, f32[512,512]{1,0:T(8,128)}, u32[]{:S(2)}) copy-start(f32[512,512]{1,0:T(8,128)} %copy-done.6) | copy-start | bytes 3145732
  270.2 10.6 %copy-start.9 = (f32[512,1024]{1,0:T(8,128)S(1)}, f32[512,1024]{1,0:T(8,128)}, u32[]{:S(2)}) copy-start(f32[512,1024]{1,0:T(8,128)} %copy-done.8) | copy-start | bytes 6291460
  270.2 10.6 %copy-start.14 = (bf16[512,512]{1,0:T(8,128)(2,1)S(1)}, bf16[512,512]{1,0:T(8,128)(2,1)}, u32[]{:S(2)}) copy-start(bf16[512,512]{1,0:T(8,128)(2,1)} %param.27) | copy-start | bytes 1572868
  270.2 12.2 %copy-start.27 = (bf16[512,512]{1,0:T(8,128)(2,1)S(1)}, bf16[512,512]{1,0:T(8,128)(2,1)}, u32[]{:S(2)}) copy-start(bf16[512,512]{1,0:T(8,128)(2,1)} %copy-done.26) | copy-start | bytes 1572868
  272.0 11.5 %collective-permute-start.7 = (bf16[32,512]{1,0:T(8,128)(2,1)S(1)}, bf16[32,512]{1,0:T(8,128)(2,1)S(1)}, u32[]{:S(2)}, u32[]{:S(2)}) collective-permute-start(bf16[32,512]{1,0:T(8,128)(2,1)S(1)} %get-tuple-element.28), channel_id=1, source_target_pairs={{0,1},{1,2},{2,3},{3,4},{4,5},{5,6},{6,7},{7,8},{8,9},{9,10},{10,1... | collective-permute-start | bytes 98312 | tf_op jit(solution)/shard_map/ppermute | solution.py:11
  274.4 9.1 %collective-permute-start.6 = (bf16[32,512]{1,0:T(8,128)(2,1)S(1)}, bf16[32,512]{1,0:T(8,128)(2,1)S(1)}, u32[]{:S(2)}, u32[]{:S(2)}) collective-permute-start(bf16[32,512]{1,0:T(8,128)(2,1)S(1)} %get-tuple-element.29), channel_id=1, source_target_pairs={{1,0},{2,1},{3,2},{4,3},{5,4},{6,5},{7,6},{8,7},{9,8},{10,9},{11,1... | collective-permute-start | bytes 98312 | tf_op jit(solution)/shard_map/ppermute | solution.py:11
  275.7 7.8 %collective-permute-start.5 = (bf16[32,512]{1,0:T(8,128)(2,1)S(1)}, bf16[32,512]{1,0:T(8,128)(2,1)S(1)}, u32[]{:S(2)}, u32[]{:S(2)}) collective-permute-start(bf16[32,512]{1,0:T(8,128)(2,1)S(1)} %get-tuple-element.30), channel_id=1, source_target_pairs={{0,16},{16,32},{32,48},{48,64},{64,80},{80,96},{96,112},{1,17},{17... | collective-permute-start | bytes 98312 | tf_op jit(solution)/shard_map/ppermute | solution.py:11
  278.8 5.2 %collective-permute-start.4 = (bf16[32,512]{1,0:T(8,128)(2,1)S(1)}, bf16[32,512]{1,0:T(8,128)(2,1)S(1)}, u32[]{:S(2)}, u32[]{:S(2)}) collective-permute-start(bf16[32,512]{1,0:T(8,128)(2,1)S(1)} %get-tuple-element.27), channel_id=1, source_target_pairs={{16,0},{32,16},{48,32},{64,48},{80,64},{96,80},{112,96},{17,1},{33... | collective-permute-start | bytes 98312 | tf_op jit(solution)/shard_map/ppermute | solution.py:11
  285.8 128.8 %copy-start.18 = (f32[512,512]{1,0:T(8,128)}, f32[512,512]{1,0:T(8,128)S(1)}, u32[]{:S(2)}) copy-start(f32[512,512]{1,0:T(8,128)S(1)} %scatter_custom_fusion.5) | copy-start | bytes 3145732
  407.2 4.8 %copy-start.17 = (f32[512,512]{1,0:T(8,128)S(1)}, f32[512,512]{1,0:T(8,128)}, u32[]{:S(2)}) copy-start(f32[512,512]{1,0:T(8,128)} %get-tuple-element.13) | copy-start | bytes 3145732
  407.2 5.9 %copy-start.13 = (f32[1024,512]{1,0:T(8,128)S(1)}, f32[1024,512]{1,0:T(8,128)}, u32[]{:S(2)}) copy-start(f32[1024,512]{1,0:T(8,128)} %get-tuple-element.14) | copy-start | bytes 6291460
  409.6 5.0 %copy-start.16 = (f32[512,512]{1,0:T(8,128)S(1)}, f32[512,512]{1,0:T(8,128)}, u32[]{:S(2)}) copy-start(f32[512,512]{1,0:T(8,128)} %get-tuple-element.15) | copy-start | bytes 3145732
  412.0 3.7 copy-start.15
  413.1 3.7 copy-start.1
Sparse Core Ops, SparseCore 0:
  240.8 166.3 all-reduce.2
where the time goes:
time: 425 us; the launch traced here: 424 us
  waiting for transfers between devices  192 us (45%)
  other arithmetic  69.8 us (16%)
  local copies, waits for them, and re-layouts  62 us (15%)
  starting transfers between devices  46.9 us (11%)
  matrix products  38 us (9%)
  between operations  14.8 us (3%)
    psum x1, waiting for transfers between devices, local(): lax.psum((source_gradient, target_gradient, edge_gradient, inner_gradient...  121 us
    all_to_all x4, waiting for transfers between devices, trade_slots(): lax.all_to_all(buffer, ('row', 'col'), split_axis=0, concat_axis=0, tiled...  70.4 us
    all_to_all x4, starting transfers between devices, trade_slots(): lax.all_to_all(buffer, ('row', 'col'), split_axis=0, concat_axis=0, tiled...  26.8 us
    ppermute x8, starting transfers between devices, passed_along(): lax.ppermute(value, axis, [(source, source + steps) for source in range(i...  20 us
    scatter-add x1, other arithmetic, local(): jax.ops.segment_sum(jax.nn.silu(message_linear), edge_target, count_rows)  14.6 us
    dot_general x6, matrix products, left_product(): lax.dot_general(first, second, (((0,), (0,)), ((), ())), preferred_elemen...  13.9 us
    scatter-add x1, other arithmetic, local(): jax.ops.segment_sum(grad_edges, edge_target, count_rows)  13.7 us
    scatter-add x1, other arithmetic, local(): jax.ops.segment_sum(grad_edges, edge_source, extended.shape[0])  13.6 us
  transfers between devices with their start and end apart: 13, of which 6 were waited for; matrix products, arithmetic and copies ran while one was open for 9% of the time, Pallas kernels for 0%

commit v1 on v0

--- a/solution.py
+++ b/solution.py
@@ -3,6 +3,7 @@
 import jax.numpy as jnp
 from jax import lax
 from jax.sharding import PartitionSpec as P
+from jax.lax import psum
 
 
 def passed_along(value, axis, steps):
@@ -141,6 +142,14 @@
     grad_targets = jax.ops.segment_sum(grad_edges, edge_target, count_rows).astype(jnp.bfloat16)
     source_gradient = left_product(extended, grad_sources)
     target_gradient = left_product(nodes, grad_targets)
+
+    def report_weights_over_axis(state):
+        link_axis = "row"
+        mesh_ax = "col"
+        for no in (mesh_ax, link_axis):
+            state = psum(state, axis_name=no)
+        return state
+
     (
         source_gradient,
         target_gradient,
@@ -148,7 +157,7 @@
         inner_gradient,
         outer_gradient,
         coarse_gradient,
-    ) = lax.psum(
+    ) = report_weights_over_axis(
         (
             source_gradient,
             target_gradient,
@@ -156,8 +165,7 @@
             inner_gradient,
             outer_gradient,
             coarse_gradient,
-        ),
-        ("row", "col"),
+        )
     )
     grad_extended = right_product(grad_sources, source_weight)
     back_blocks = grad_extended[count_rows:].astype(jnp.bfloat16).reshape(4, halo_rows, width)

time: 425 us -> 492 us (1.16)
  waiting for transfers between devices: 192 us -> 255 us
    psum x1 -> x2, waiting for transfers between devices: 121 us -> 187 us  [report_weights_over_axis(): state = psum(state, axis_name=no)]
  transfers between devices with their start and end apart: 13 -> 14, of which waited for: 6 -> 7; matrix products, arithmetic and copies ran while one was open for 9% -> 7% of each run, Pallas kernels for 0% -> 0%
where the time goes in v1:
time: 492 us; the launch traced here: 491 us
  waiting for transfers between devices  255 us (52%)
  other arithmetic  69.7 us (14%)
  local copies, waits for them, and re-layouts  62 us (13%)
  starting transfers between devices  51.4 us (10%)
  matrix products  37.9 us (8%)
  between operations  14.8 us (3%)
    psum x2, waiting for transfers between devices, report_weights_over_axis(): state = psum(state, axis_name=no)  187 us
    all_to_all x4, waiting for transfers between devices, trade_slots(): lax.all_to_all(buffer, ('row', 'col'), split_axis=0, concat_axis=0, tiled...  66.4 us
    all_to_all x4, starting transfers between devices, trade_slots(): lax.all_to_all(buffer, ('row', 'col'), split_axis=0, concat_axis=0, tiled...  30.4 us
    ppermute x8, starting transfers between devices, passed_along(): lax.ppermute(value, axis, [(source, source + steps) for source in range(i...  20.8 us
    scatter-add x1, other arithmetic, local(): jax.ops.segment_sum(jax.nn.silu(message_linear), edge_target, count_rows)  14.6 us
    dot_general x6, matrix products, left_product(): lax.dot_general(first, second, (((0,), (0,)), ((), ())), preferred_elemen...  13.9 us
    scatter-add x1, other arithmetic, local(): jax.ops.segment_sum(grad_edges, edge_target, count_rows)  13.7 us
    scatter-add x1, other arithmetic, local(): jax.ops.segment_sum(grad_edges, edge_source, extended.shape[0])  13.6 us
  transfers between devices with their start and end apart: 14, of which 7 were waited for; matrix products, arithmetic and copies ran while one was open for 7% of the time, Pallas kernels for 0%

profile of v1, /device:TPU:1, one launch (start us, length us, event | category | flops | bytes accessed | tf_op | source)
XLA Modules:
  0.0 490.6 jit_solution(6487926562509666258)
XLA Ops:
  8.1 1.7 gather_fusion.3
  9.9 4.9 %collective-permute-start = (bf16[32,512]{1,0:T(8,128)(2,1)S(1)}, bf16[32,512]{1,0:T(8,128)(2,1)S(1)}, u32[]{:S(2)}, u32[]{:S(2)}) collective-permute-start(bf16[32,512]{1,0:T(8,128)(2,1)S(1)} %broadcast_select_fusion.4), channel_id=1, source_target_pairs={{0,16},{16,32},{32,48},{48,64},{64,80},{80,96},{96,112},{1,17},{17... | collective-permute-start | bytes 98312 | tf_op jit(solution)/shard_map/ppermute | solution.py:12
  14.8 1.7 gather_fusion.4
  16.7 1.9 collective-permute-start.1
  18.6 1.7 gather_fusion.5
  20.4 3.2 collective-permute-start.2
  23.6 1.7 gather_fusion.6
  25.5 1.3 collective-permute-start.3
  27.5 1.3 compare_and_fusion
  28.8 1.6 fusion.57
  32.1 8.9 %gather_fusion.1 = f32[2048,512]{1,0:T(8,128)} fusion(f32[512,512]{1,0:T(8,128)S(1)} %fusion.57, s32[2048]{0:T(1024)S(1)} %get-tuple-element.52), kind=kCustom, calls=%fused_computation.9 | custom fusion | bytes 8396800 | tf_op jit(solution)/shard_map/jit(_take)/gather | solution.py:91
  41.1 1.5 fusion.56
  42.6 9.0 %gather_fusion = f32[2048,512]{1,0:T(8,128)} fusion(f32[640,512]{1,0:T(8,128)S(1)} %fusion.56, s32[2048]{0:T(1024)S(1)} %get-tuple-element.51), kind=kCustom, calls=%fused_computation.8 | custom fusion | bytes 8396800 | tf_op jit(solution)/shard_map/jit(_take)/gather | solution.py:91
  51.6 4.2 multiply_convert_fusion.1
  55.9 1.3 copy-done.5
  57.1 3.3 fusion.58
  60.5 14.6 %scatter_custom_fusion = f32[512,512]{1,0:T(8,128)S(1)} fusion(s32[2048]{0:T(1024)} %param.22, f32[2048,512]{1,0:T(8,128)} %fusion.58, f32[]{:T(128)} %constant.62.clone.1, f32[]{:T(128)} %constant.52.clone.1), kind=kCustom, calls=%fused_computation.19 | custom fusion | flops 5242880 | bytes 5243904 | tf_op jit(solution)/shard_map/scatter-add | solution.py:96
  77.2 3.6 scatter_custom_fusion.1
  80.8 11.6 %all-to-all-start = ((bf16[128,8,512]{2,1,0:T(8,128)(2,1)}), bf16[128,8,512]{2,1,0:T(8,128)(2,1)S(1)}, u32[]{:S(2)}, u32[]{:S(2)}) async-start(bf16[128,8,512]{2,1,0:T(8,128)(2,1)} %bitcast.5), calls=%async_computation | async-start | bytes 2097152 | tf_op jit(solution)/shard_map/all_to_all | solution.py:46
  92.4 4.0 scatter_custom_fusion.2
  96.5 14.7 %all-to-all-done = bf16[128,8,512]{2,1,0:T(8,128)(2,1)S(1)} async-done(((bf16[128,8,512]{2,1,0:T(8,128)(2,1)}), bf16[128,8,512]{2,1,0:T(8,128)(2,1)S(1)}, u32[]{:S(2)}, u32[]{:S(2)}) %all-to-all-start) | async-done | bytes 1048608 | tf_op jit(solution)/shard_map/all_to_all | solution.py:46
  111.2 5.7 %all-to-all-start.2 = ((bf16[128,8,512]{2,1,0:T(8,128)(2,1)}), bf16[128,8,512]{2,1,0:T(8,128)(2,1)}, u32[]{:S(2)}, u32[]{:S(2)}) async-start(bf16[128,8,512]{2,1,0:T(8,128)(2,1)} %bitcast.9), calls=%async_computation.2 | async-start | bytes 2097152 | tf_op jit(solution)/shard_map/all_to_all | solution.py:46
  117.9 1.4 multiply_convert_fusion.3
  119.2 16.3 %all-to-all-done.2 = bf16[128,8,512]{2,1,0:T(8,128)(2,1)} async-done(((bf16[128,8,512]{2,1,0:T(8,128)(2,1)}), bf16[128,8,512]{2,1,0:T(8,128)(2,1)}, u32[]{:S(2)}, u32[]{:S(2)}) %all-to-all-start.2) | async-done | bytes 1048608 | tf_op jit(solution)/shard_map/all_to_all | solution.py:46
  135.6 1.5 fusion.8
  137.8 1.4 fusion.6
  139.1 4.0 gather_fusion.9
  143.1 5.1 %gather_fusion.7 = bf16[1024,512]{1,0:T(8,128)(2,1)} fusion(bf16[128,512]{1,0:T(8,128)(2,1)S(1)} %get-tuple-element.47, s32[1024]{0:T(1024)S(1)} %maximum_clamp_fusion), kind=kCustom, calls=%fused_computation.1.clone | custom fusion | bytes 2101248 | tf_op jit(solution)/shard_map/jit(_take)/gather | solution.py:58
  148.2 2.9 fusion.12
  151.1 4.8 all-to-all-start.3
  156.0 2.3 fusion.61
  158.3 16.6 %all-to-all-done.3 = bf16[128,8,512]{2,1,0:T(8,128)(2,1)S(1)} async-done(((bf16[128,8,512]{2,1,0:T(8,128)(2,1)}), bf16[128,8,512]{2,1,0:T(8,128)(2,1)S(1)}, u32[]{:S(2)}, u32[]{:S(2)}) %all-to-all-start.3) | async-done | bytes 1048608 | tf_op jit(solution)/shard_map/all_to_all | solution.py:46
  174.9 2.6 gather_fusion.10
  177.5 2.4 fusion.5
  180.7 1.3 copy-done.8
  182.1 9.2 %gather_fusion.2 = bf16[2048,512]{1,0:T(8,128)(2,1)} fusion(bf16[512,512]{1,0:T(8,128)(2,1)S(1)} %slice.97, s32[2048]{0:T(1024)S(1)} %get-tuple-element.52), kind=kCustom, calls=%fused_computation.10 | custom fusion | bytes 4202496 | tf_op jit(solution)/shard_map/jit(_take)/gather | solution.py:135
  191.3 3.8 multiply_convert_fusion
  195.2 1.3 copy-done.10
  197.4 4.3 multiply_multiply_fusion
  201.7 13.6 %scatter_custom_fusion.4 = f32[640,512]{1,0:T(8,128)S(1)} fusion(s32[2048]{0:T(1024)} %param.21, f32[2048,512]{1,0:T(8,128)} %multiply_multiply_fusion, f32[]{:T(128)} %constant.52.clone.1), kind=kCustom, calls=%fused_computation.59 | custom fusion | flops 1048576 | bytes 1311232 | tf_op jit(solution)/shard_map/scatter-add | solution.py:139
  215.2 13.7 %scatter_custom_fusion.3 = f32[512,512]{1,0:T(8,128)S(1)} fusion(s32[2048]{0:T(1024)} %param.22, f32[2048,512]{1,0:T(8,128)} %multiply_multiply_fusion, f32[]{:T(128)} %constant.52.clone.1), kind=kCustom, calls=%fused_computation.73 | custom fusion | flops 1048576 | bytes 1049088 | tf_op jit(solution)/shard_map/scatter-add | solution.py:142
  229.0 4.9 fusion.60
  233.9 2.1 fusion.15
  236.0 1.7 fusion.51
  237.7 1.6 fusion.27
  239.2 1.5 convolution_bitcast_fusion
  240.8 127.6 %all-reduce.5.cloned.1.call-done = (f32[512,512]{1,0:T(8,128)}, f32[512,512]{1,0:T(8,128)}, f32[512,512]{1,0:T(8,128)}, f32[1024,512]{1,0:T(8,128)}, f32[512,512]{1,0:T(8,128)}, /*index=5*/f32[512,512]{1,0:T(8,128)}) async-done(((f32[512,512]{1,0:T(8,128)}, f32[512,512]{1,0:T(8,128)}, f32[512,512]{1,0:T(8,128)}, f32[1024,512]{1,0:T(8,128)}, f32[512,512]{1,0:T(8,128)}, /*index=5*/f32[512,512]{1,0:T(8,128)}), ...) | async-done | bytes 7340048 | tf_op jit(solution)/shard_map/psum | solution.py:150
  368.4 8.3 %all-to-all-start.1 = ((bf16[128,8,512]{2,1,0:T(8,128)(2,1)}), bf16[128,8,512]{2,1,0:T(8,128)(2,1)S(1)}, u32[]{:S(2)}, u32[]{:S(2)}) async-start(bf16[128,8,512]{2,1,0:T(8,128)(2,1)} %get-tuple-element.40), calls=%async_computation.1 | async-start | bytes 2097152 | tf_op jit(solution)/shard_map/all_to_all | solution.py:46
  376.8 18.7 %all-to-all-done.1 = bf16[128,8,512]{2,1,0:T(8,128)(2,1)S(1)} async-done(((bf16[128,8,512]{2,1,0:T(8,128)(2,1)}), bf16[128,8,512]{2,1,0:T(8,128)(2,1)S(1)}, u32[]{:S(2)}, u32[]{:S(2)}) %all-to-all-start.1) | async-done | bytes 1048608 | tf_op jit(solution)/shard_map/all_to_all | solution.py:46
  395.6 2.0 gather_fusion.8
  397.6 1.7 fusion.55
  399.4 2.1 collective-permute-start.7
  401.5 1.3 collective-permute-start.6
  402.8 4.2 collective-permute-start.5
  407.0 1.9 collective-permute-start.4
  409.0 1.6 fusion.3
  411.7 1.4 collective-permute-done.4
  413.1 1.8 scatter_custom_fusion.5
  414.8 59.3 %all-reduce.7.cloned.1.call-done = (f32[512,512]{1,0:T(8,128)}, f32[512,512]{1,0:T(8,128)}, f32[512,512]{1,0:T(8,128)}, f32[1024,512]{1,0:T(8,128)}, f32[512,512]{1,0:T(8,128)}, /*index=5*/f32[512,512]{1,0:T(8,128)}) async-done(((f32[512,512]{1,0:T(8,128)}, f32[512,512]{1,0:T(8,128)}, f32[512,512]{1,0:T(8,128)}, f32[1024,512]{1,0:T(8,128)}, f32[512,512]{1,0:T(8,128)}, /*index=5*/f32[512,512]{1,0:T(8,128)}), ...) | async-done | bytes 7340048 | tf_op jit(solution)/shard_map/psum | solution.py:150
  474.2 2.4 broadcast_multiply_fusion.5
  476.6 2.4 broadcast_multiply_fusion.4
  480.1 1.5 broadcast_multiply_fusion
  481.6 1.1 broadcast_multiply_fusion.2
  482.7 1.1 broadcast_multiply_fusion.1
  (129 shorter events, 11.7 us)
Async XLA Ops:
  7.2 68.0 %copy-start = (bf16[1024,512]{1,0:T(8,128)(2,1)S(1)}, bf16[1024,512]{1,0:T(8,128)(2,1)}, u32[]{:S(2)}) copy-start(bf16[1024,512]{1,0:T(8,128)(2,1)} %param.29) | copy-start | bytes 3145732
  7.2 24.9 %copy-start.4 = (bf16[512,512]{1,0:T(8,128)(2,1)S(1)}, bf16[512,512]{1,0:T(8,128)(2,1)}, u32[]{:S(2)}) copy-start(bf16[512,512]{1,0:T(8,128)(2,1)} %param.19) | copy-start | bytes 1572868
  7.2 24.3 %copy-start.39 = (s32[512]{0:T(512)S(1)}, s32[512]{0:T(512)}, u32[]{:S(2)}) copy-start(s32[512]{0:T(512)} %param.24) | copy-start | bytes 6148
  9.9 31.1 %collective-permute-start = (bf16[32,512]{1,0:T(8,128)(2,1)S(1)}, bf16[32,512]{1,0:T(8,128)(2,1)S(1)}, u32[]{:S(2)}, u32[]{:S(2)}) collective-permute-start(bf16[32,512]{1,0:T(8,128)(2,1)S(1)} %broadcast_select_fusion.4), channel_id=1, source_target_pairs={{0,16},{16,32},{32,48},{48,64},{64,80},{80,96},{96,112},{1,17},{17... | collective-permute-start | bytes 98312 | tf_op jit(solution)/shard_map/ppermute | solution.py:12
  16.7 24.4 %collective-permute-start.1 = (bf16[32,512]{1,0:T(8,128)(2,1)S(1)}, bf16[32,512]{1,0:T(8,128)(2,1)S(1)}, u32[]{:S(2)}, u32[]{:S(2)}) collective-permute-start(bf16[32,512]{1,0:T(8,128)(2,1)S(1)} %broadcast_select_fusion.3), channel_id=1, source_target_pairs={{16,0},{32,16},{48,32},{64,48},{80,64},{96,80},{112,96},{17,1},{33... | collective-permute-start | bytes 98312 | tf_op jit(solution)/shard_map/ppermute | solution.py:12
  20.4 20.6 %collective-permute-start.2 = (bf16[32,512]{1,0:T(8,128)(2,1)S(1)}, bf16[32,512]{1,0:T(8,128)(2,1)S(1)}, u32[]{:S(2)}, u32[]{:S(2)}) collective-permute-start(bf16[32,512]{1,0:T(8,128)(2,1)S(1)} %broadcast_select_fusion.2), channel_id=1, source_target_pairs={{0,1},{1,2},{2,3},{3,4},{4,5},{5,6},{6,7},{7,8},{8,9},{9,10},{10,1... | collective-permute-start | bytes 98312 | tf_op jit(solution)/shard_map/ppermute | solution.py:12
  25.5 15.6 %collective-permute-start.3 = (bf16[32,512]{1,0:T(8,128)(2,1)S(1)}, bf16[32,512]{1,0:T(8,128)(2,1)S(1)}, u32[]{:S(2)}, u32[]{:S(2)}) collective-permute-start(bf16[32,512]{1,0:T(8,128)(2,1)S(1)} %broadcast_select_fusion.1), channel_id=1, source_target_pairs={{1,0},{2,1},{3,2},{4,3},{5,4},{6,5},{7,6},{8,7},{9,8},{10,9},{11,1... | collective-permute-start | bytes 98312 | tf_op jit(solution)/shard_map/ppermute | solution.py:12
  51.6 5.6 %copy-start.19 = (bf16[512,512]{1,0:T(8,128)(2,1)S(1)}, bf16[512,512]{1,0:T(8,128)(2,1)}, u32[]{:S(2)}) copy-start(bf16[512,512]{1,0:T(8,128)(2,1)} %param.28) | copy-start | bytes 1572868
  55.8 1.3 copy-start.5
  75.1 1.2 copy-start.40
  75.2 1.5 copy-start.22
  76.2 1.0 copy-start.42
  76.2 20.1 %copy-start.30 = (s32[1,1024]{1,0:T(1,128)S(1)}, s32[1,1024]{1,0:T(1,128)}, u32[]{:S(2)}) copy-start(s32[1,1024]{1,0:T(1,128)} %param.25) | copy-start | bytes 12292
  77.2 3.6 copy-start.26
  80.8 30.4 %all-to-all-start = ((bf16[128,8,512]{2,1,0:T(8,128)(2,1)}), bf16[128,8,512]{2,1,0:T(8,128)(2,1)S(1)}, u32[]{:S(2)}, u32[]{:S(2)}) async-start(bf16[128,8,512]{2,1,0:T(8,128)(2,1)} %bitcast.5), calls=%async_computation | async-start | bytes 2097152 | tf_op jit(solution)/shard_map/all_to_all | solution.py:46
  111.2 24.4 %all-to-all-start.2 = ((bf16[128,8,512]{2,1,0:T(8,128)(2,1)}), bf16[128,8,512]{2,1,0:T(8,128)(2,1)}, u32[]{:S(2)}, u32[]{:S(2)}) async-start(bf16[128,8,512]{2,1,0:T(8,128)(2,1)} %bitcast.9), calls=%async_computation.2 | async-start | bytes 2097152 | tf_op jit(solution)/shard_map/all_to_all | solution.py:46
  117.0 18.6 %copy-start.41 = (f32[128]{0:T(128)}, f32[128]{0:T(128)S(1)}, u32[]{:S(2)}) copy-start(f32[128]{0:T(128)S(1)} %broadcast_maximum_fusion) | copy-start | bytes 1540
  117.9 19.2 %copy-start.28 = (bf16[128,512]{1,0:T(8,128)(2,1)}, bf16[128,512]{1,0:T(8,128)(2,1)S(1)}, u32[]{:S(2)}) copy-start(bf16[128,512]{1,0:T(8,128)(2,1)S(1)} %fusion.7) | copy-start | bytes 393220
  137.1 0.7 copy-start.29
  143.1 5.1 %copy-start.37 = (pred[1024]{0:T(1024)(128)(4,1)S(1)}, pred[1024]{0:T(1024)(128)(4,1)}, u32[]{:S(2)}) copy-start(pred[1024]{0:T(1024)(128)(4,1)} %get-tuple-element.37) | copy-start | bytes 3076
  143.1 5.1 %copy-start.38 = (pred[1024]{0:T(1024)(128)(4,1)S(1)}, pred[1024]{0:T(1024)(128)(4,1)}, u32[]{:S(2)}) copy-start(pred[1024]{0:T(1024)(128)(4,1)} %get-tuple-element.38) | copy-start | bytes 3076
  148.2 7.8 %copy-start.34 = (s32[512]{0:T(512)S(1)}, s32[512]{0:T(512)}, u32[]{:S(2)}) copy-start(s32[512]{0:T(512)} %get-tuple-element.24) | copy-start | bytes 6148
  151.1 26.4 %copy-start.35 = (pred[512]{0:T(512)(128)(4,1)S(1)}, pred[512]{0:T(512)(128)(4,1)}, u32[]{:S(2)}) copy-start(pred[512]{0:T(512)(128)(4,1)} %get-tuple-element.23) | copy-start | bytes 1540
  151.1 23.8 %all-to-all-start.3 = ((bf16[128,8,512]{2,1,0:T(8,128)(2,1)}), bf16[128,8,512]{2,1,0:T(8,128)(2,1)S(1)}, u32[]{:S(2)}, u32[]{:S(2)}) async-start(bf16[128,8,512]{2,1,0:T(8,128)(2,1)} %get-tuple-element.39), calls=%async_computation.3 | async-start | bytes 2097152 | tf_op jit(solution)/shard_map/all_to_all | solution.py:46
  155.9 212.5 %all-reduce.5.cloned.1.call-start = ((), (), s32[]{:S(2)}) async-start(), calls=%async_computation.4 | async-start | bytes 14680064 | tf_op jit(solution)/shard_map/psum | solution.py:150
  179.9 0.8 copy-start.24
  180.7 1.3 copy-start.8
  182.1 9.2 %copy-start.31 = (pred[2048]{0:T(1024)(128)(4,1)S(1)}, pred[2048]{0:T(1024)(128)(4,1)}, u32[]{:S(2)}) copy-start(pred[2048]{0:T(1024)(128)(4,1)} %get-tuple-element.53) | copy-start | bytes 6148
  182.1 14.4 %copy-start.20 = (bf16[512,512]{1,0:T(8,128)(2,1)S(1)}, bf16[512,512]{1,0:T(8,128)(2,1)}, u32[]{:S(2)}) copy-start(bf16[512,512]{1,0:T(8,128)(2,1)} %param.28) | copy-start | bytes 1572868
  191.3 5.1 %copy-start.2 = (f32[2048,512]{1,0:T(8,128)S(1)}, f32[2048,512]{1,0:T(8,128)}, u32[]{:S(2)}) copy-start(f32[2048,512]{1,0:T(8,128)} %gather_fusion.1) | copy-start | bytes 12582916
  191.3 6.1 %copy-start.3 = (f32[2048,512]{1,0:T(8,128)S(1)}, f32[2048,512]{1,0:T(8,128)}, u32[]{:S(2)}) copy-start(f32[2048,512]{1,0:T(8,128)} %gather_fusion) | copy-start | bytes 12582916
  191.3 6.1 %copy-start.32 = (pred[2048]{0:T(1024)(128)(4,1)S(1)}, pred[2048]{0:T(1024)(128)(4,1)}, u32[]{:S(2)}) copy-start(pred[2048]{0:T(1024)(128)(4,1)} %get-tuple-element.54) | copy-start | bytes 6148
  195.1 1.3 copy-start.10
  229.0 10.3 %copy-start.6 = (f32[512,512]{1,0:T(8,128)}, f32[512,512]{1,0:T(8,128)S(1)}, u32[]{:S(2)}) copy-start(f32[512,512]{1,0:T(8,128)S(1)} %scatter_custom_fusion.3) | copy-start | bytes 3145732
  229.0 4.9 %copy-start.23 = (bf16[512,512]{1,0:T(8,128)(2,1)S(1)}, bf16[512,512]{1,0:T(8,128)(2,1)}, u32[]{:S(2)}) copy-start(bf16[512,512]{1,0:T(8,128)(2,1)} %copy-done.22) | copy-start | bytes 1572868
  229.0 4.9 %copy-start.25 = (bf16[512,512]{1,0:T(8,128)(2,1)S(1)}, bf16[512,512]{1,0:T(8,128)(2,1)}, u32[]{:S(2)}) copy-start(bf16[512,512]{1,0:T(8,128)(2,1)} %copy-done.24) | copy-start | bytes 1572868
  229.0 7.0 %copy-start.11 = (bf16[512,512]{1,0:T(8,128)(2,1)S(1)}, bf16[512,512]{1,0:T(8,128)(2,1)}, u32[]{:S(2)}) copy-start(bf16[512,512]{1,0:T(8,128)(2,1)} %gather_fusion.10) | copy-start | bytes 1572868
  229.0 7.0 %copy-start.21 = (bf16[512,512]{1,0:T(8,128)(2,1)S(1)}, bf16[512,512]{1,0:T(8,128)(2,1)}, u32[]{:S(2)}) copy-start(bf16[512,512]{1,0:T(8,128)(2,1)} %param.20) | copy-start | bytes 1572868
  229.0 7.0 %copy-start.36 = (pred[512]{0:T(512)(128)(4,1)S(1)}, pred[512]{0:T(512)(128)(4,1)}, u32[]{:S(2)}) copy-start(pred[512]{0:T(512)(128)(4,1)} %get-tuple-element.23) | copy-start | bytes 1540
  229.0 7.0 %copy-start.43 = (f32[512,512]{1,0:T(8,128)S(1)}, f32[512,512]{1,0:T(8,128)}, u32[]{:S(2)}) copy-start(f32[512,512]{1,0:T(8,128)} %copy-done.42) | copy-start | bytes 3145732
  240.7 233.4 %all-reduce.7.cloned.1.call-start = ((), (), s32[]{:S(2)}) async-start(), calls=%async_computation.5 | async-start | bytes 14680064 | tf_op jit(solution)/shard_map/psum | solution.py:150
  368.4 8.4 %copy-start.33 = (s32[1,4,32]{2,1,0:T(4,128)S(1)}, s32[1,4,32]{2,1,0:T(4,128)}, u32[]{:S(2)}) copy-start(s32[1,4,32]{2,1,0:T(4,128)} %param.23) | copy-start | bytes 1540
  368.4 27.2 %all-to-all-start.1 = ((bf16[128,8,512]{2,1,0:T(8,128)(2,1)}), bf16[128,8,512]{2,1,0:T(8,128)(2,1)S(1)}, u32[]{:S(2)}, u32[]{:S(2)}) async-start(bf16[128,8,512]{2,1,0:T(8,128)(2,1)} %get-tuple-element.40), calls=%async_computation.1 | async-start | bytes 2097152 | tf_op jit(solution)/shard_map/all_to_all | solution.py:46
  395.6 13.4 %copy-start.12 = (bf16[512,512]{1,0:T(8,128)(2,1)S(1)}, bf16[512,512]{1,0:T(8,128)(2,1)}, u32[]{:S(2)}) copy-start(bf16[512,512]{1,0:T(8,128)(2,1)} %gather_fusion.10) | copy-start | bytes 1572868
  397.5 11.4 %copy-start.7 = (f32[512,512]{1,0:T(8,128)S(1)}, f32[512,512]{1,0:T(8,128)}, u32[]{:S(2)}) copy-start(f32[512,512]{1,0:T(8,128)} %copy-done.6) | copy-start | bytes 3145732
  397.6 11.4 %copy-start.9 = (f32[512,1024]{1,0:T(8,128)S(1)}, f32[512,1024]{1,0:T(8,128)}, u32[]{:S(2)}) copy-start(f32[512,1024]{1,0:T(8,128)} %copy-done.8) | copy-start | bytes 6291460
  397.6 11.4 %copy-start.14 = (bf16[512,512]{1,0:T(8,128)(2,1)S(1)}, bf16[512,512]{1,0:T(8,128)(2,1)}, u32[]{:S(2)}) copy-start(bf16[512,512]{1,0:T(8,128)(2,1)} %param.27) | copy-start | bytes 1572868
  397.6 13.0 %copy-start.27 = (bf16[512,512]{1,0:T(8,128)(2,1)S(1)}, bf16[512,512]{1,0:T(8,128)(2,1)}, u32[]{:S(2)}) copy-start(bf16[512,512]{1,0:T(8,128)(2,1)} %copy-done.26) | copy-start | bytes 1572868
  399.4 12.3 %collective-permute-start.7 = (bf16[32,512]{1,0:T(8,128)(2,1)S(1)}, bf16[32,512]{1,0:T(8,128)(2,1)S(1)}, u32[]{:S(2)}, u32[]{:S(2)}) collective-permute-start(bf16[32,512]{1,0:T(8,128)(2,1)S(1)} %get-tuple-element.34), channel_id=1, source_target_pairs={{0,1},{1,2},{2,3},{3,4},{4,5},{5,6},{6,7},{7,8},{8,9},{9,10},{10,1... | collective-permute-start | bytes 98312 | tf_op jit(solution)/shard_map/ppermute | solution.py:12
  401.5 10.1 %collective-permute-start.6 = (bf16[32,512]{1,0:T(8,128)(2,1)S(1)}, bf16[32,512]{1,0:T(8,128)(2,1)S(1)}, u32[]{:S(2)}, u32[]{:S(2)}) collective-permute-start(bf16[32,512]{1,0:T(8,128)(2,1)S(1)} %get-tuple-element.35), channel_id=1, source_target_pairs={{1,0},{2,1},{3,2},{4,3},{5,4},{6,5},{7,6},{8,7},{9,8},{10,9},{11,1... | collective-permute-start | bytes 98312 | tf_op jit(solution)/shard_map/ppermute | solution.py:12
  402.8 8.9 %collective-permute-start.5 = (bf16[32,512]{1,0:T(8,128)(2,1)S(1)}, bf16[32,512]{1,0:T(8,128)(2,1)S(1)}, u32[]{:S(2)}, u32[]{:S(2)}) collective-permute-start(bf16[32,512]{1,0:T(8,128)(2,1)S(1)} %get-tuple-element.36), channel_id=1, source_target_pairs={{0,16},{16,32},{32,48},{48,64},{64,80},{80,96},{96,112},{1,17},{17... | collective-permute-start | bytes 98312 | tf_op jit(solution)/shard_map/ppermute | solution.py:12
  407.0 6.0 %collective-permute-start.4 = (bf16[32,512]{1,0:T(8,128)(2,1)S(1)}, bf16[32,512]{1,0:T(8,128)(2,1)S(1)}, u32[]{:S(2)}, u32[]{:S(2)}) collective-permute-start(bf16[32,512]{1,0:T(8,128)(2,1)S(1)} %get-tuple-element.33), channel_id=1, source_target_pairs={{16,0},{32,16},{48,32},{64,48},{80,64},{96,80},{112,96},{17,1},{33... | collective-permute-start | bytes 98312 | tf_op jit(solution)/shard_map/ppermute | solution.py:12
  414.8 66.8 %copy-start.18 = (f32[512,512]{1,0:T(8,128)}, f32[512,512]{1,0:T(8,128)S(1)}, u32[]{:S(2)}) copy-start(f32[512,512]{1,0:T(8,128)S(1)} %scatter_custom_fusion.5) | copy-start | bytes 3145732
  474.2 4.8 copy-start.17
  474.2 5.9 %copy-start.13 = (f32[1024,512]{1,0:T(8,128)S(1)}, f32[1024,512]{1,0:T(8,128)}, u32[]{:S(2)}) copy-start(f32[1024,512]{1,0:T(8,128)} %get-tuple-element.20) | copy-start | bytes 6291460
  476.6 5.0 %copy-start.16 = (f32[512,512]{1,0:T(8,128)S(1)}, f32[512,512]{1,0:T(8,128)}, u32[]{:S(2)}) copy-start(f32[512,512]{1,0:T(8,128)} %get-tuple-element.21) | copy-start | bytes 3145732
  479.0 3.7 copy-start.15
  480.1 3.7 copy-start.1
Sparse Core Ops, SparseCore 0:
  240.8 127.4 all-reduce.4
  371.2 102.9 all-reduce.6
